TPU v7x, 32 devices: a whole 2x2x4 slice. The times are simulated.
32 devices in a mesh: dp: 2 (over core), tok: 4 (over y, x), exp: 4 (over z).
Axes of the slice: x: 2, y: 2, z: 4, core: 2. Of those that a mesh axis runs over, the one named last changes fastest.
Arguments:
- tokens: bfloat16 [16, 1024, 1280], P(('dp', 'exp'), 'tok'), parts along dimension 0, may hold values from -64 to 64
- router: bfloat16 [1280, 64], P(None, 'dp'), parts along dimension 1, may hold values from -1 to 1
- image_counts: int32 [16, 16], P(('dp', 'exp')), parts along dimension 0, may hold values from 1 to 64, as said below
- image_offsets: int32 [16, 16], P(('dp', 'exp')), parts along dimension 0, may hold values from 0 to 960, as said below
- expert_in: bfloat16 [32, 1280, 4096], P('exp', None, 'tok'), may hold values from -0.15625 to 0.15625
- expert_out: bfloat16 [32, 4096, 1280], P('exp', 'tok'), may hold values from -0.09375 to 0.09375
Outputs:
- moe_out: bfloat16 [16, 1024, 1280], P(('dp', 'exp'), 'tok'), parts along dimension 0
There are 2 independent parts, one for each index of `dp`. A program takes and returns all parts, laid end to end along the dimension named above; an argument that names none is the same for every part. Nothing has to cross between parts.
Inputs may be any that keep to these rules, and one draw needn't show every extreme that they name: Each image of a sequence covers image_counts positions from its image_offsets; the images of one sequence are disjoint, in order of rising offsets, and lie inside the sequence of 1024 positions; the last image of every sequence has 1024 // 16 positions. `image_offsets`: offsets rise along each sequence; the last image of every sequence ends at the sequence's end.
All inputs are finite; a program needn't handle non-finite values.
Results may differ from a plain program's by a relative error of at most 0.012.
Values may be sent and summed in bfloat16 or wider, within the bound.
No kernel may reach another device: no remote copies, remote signals or barrier semaphores. Data moves between devices by JAX's collectives and lax.ppermute only.
A program may use at most 128 MiB of HBM per device.

v0:
```python
import jax
import jax.numpy as jnp
from jax import lax
from jax.sharding import PartitionSpec as P


def combined_all(part, axis, combine):
    gathered = jax.tree.map(lambda a: lax.all_gather(a, axis), part)

    def take(source):
        return jax.tree.map(lambda a: lax.dynamic_index_in_dim(a, source, 0, False), gathered)

    return lax.fori_loop(
        1, lax.axis_size(axis), lambda source, state: combine(state, take(source)), take(0)
    )


def merge_parts(earlier, later_part):
    top_value = jnp.maximum(earlier[0], later_part[0])
    first_scale = jnp.exp(earlier[0] - top_value)
    second_scale = jnp.exp(later_part[0] - top_value)
    totals = earlier[1] * first_scale + later_part[1] * second_scale
    slot_sums = earlier[2] * first_scale[..., None] + later_part[2] * second_scale[..., None]
    return (top_value, totals, slot_sums)


def shards(tokens, router, image_counts, image_offsets, expert_in, expert_out):
    block_len = tokens.shape[1]
    where_at = lax.axis_index("tok") * block_len + jnp.arange(block_len, dtype=jnp.int32)
    image_ends = image_offsets + image_counts
    inside = (where_at[None, :, None] >= image_offsets[:, None, :]) & (
        where_at[None, :, None] < image_ends[:, None, :]
    )
    live_mask = jnp.any(inside, axis=-1)
    logits = jnp.einsum("bnd,ds->bns", tokens, router, preferred_element_type=jnp.float32)
    local_peak = jnp.max(jnp.where(live_mask[..., None], logits, -1e30), axis=1)
    weights = jnp.where(live_mask[..., None], jnp.exp(logits - local_peak[:, None, :]), 0.0)
    totals = jnp.sum(weights, axis=1)
    slot_sums = jnp.einsum(
        "bns,bnd->bsd", weights.astype(jnp.bfloat16), tokens, preferred_element_type=jnp.float32
    )
    totals, slot_sums = (totals, slot_sums)
    column_peak, totals, slot_sums = combined_all(
        (local_peak, totals, slot_sums), "tok", merge_parts
    )
    slot_in = (slot_sums / totals[..., None]).astype(jnp.bfloat16)
    owned_slots = lax.all_to_all(slot_in, "exp", split_axis=1, concat_axis=0, tiled=True)
    hidden = jax.nn.gelu(
        jnp.einsum("bed,edf->bef", owned_slots, expert_in, preferred_element_type=jnp.float32),
        approximate=False,
    ).astype(jnp.bfloat16)
    partial_out = jnp.einsum("bef,efd->bed", hidden, expert_out, preferred_element_type=jnp.float32)
    summed = lax.psum(partial_out, "tok")
    slot_out = lax.all_to_all(
        summed.astype(jnp.bfloat16), "exp", split_axis=0, concat_axis=1, tiled=True
    )
    combine_weights = jax.nn.softmax(logits, axis=-1).astype(jnp.bfloat16)
    mixed_out = jnp.einsum(
        "bns,bsd->bnd", combine_weights, slot_out, preferred_element_type=jnp.float32
    )
    return jnp.where(live_mask[..., None], mixed_out, 0.0).astype(jnp.bfloat16)


def solution(mesh):
    placed = (
        P(("dp", "exp"), "tok", None),
        P(None, "dp"),
        P(("dp", "exp"), None),
        P(("dp", "exp"), None),
        P("exp", None, "tok"),
        P("exp", "tok", None),
    )
    return jax.shard_map(
        shards, mesh=mesh, in_specs=placed, out_specs=P(("dp", "exp"), "tok", None), check_vma=False
    )
```

profile of v0, /device:TPU:0, one launch (start us, length us, event | category | flops | bytes accessed | tf_op | source)
XLA Modules:
  0.0 114.1 jit_solution(2261706719610102142)
XLA Ops:
  6.5 0.0 copy-start
  6.5 0.0 all-gather.7.cloned.1.call-start
  6.5 0.8 add.77
  7.3 0.8 and_reduce_fusion
  8.1 0.0 copy-done
  8.1 1.5 %select_reduce_fusion = (f32[2,32]{1,0:T(2,128)S(1)}, f32[2,256,32]{1,2,0:T(8,128)S(1)}) fusion(pred[2,256]{1,0:T(4,128)(4,1)S(1)} %and_reduce_fusion, bf16[2,256,1280]{2,1,0:T(8,128)(2,1)S(1)} %copy-done, bf16[1280,32]{0,1:T(8,128)(2,1)} %param.9), kind=kOutput, calls=%fused_computation.76 | convolution fusion | flops 41975744 | bytes 1458944 | tf_op jit(solution)/shard_map/bnd,ds->bns/dot_general | solution.py:35
  9.6 1.1 fusion.62
  10.7 0.0 all-gather.7.cloned.1.call-update
  10.7 0.2 fusion.61
  10.9 9.6 %all-gather.4 = f32[4,2,32]{2,1,0:T(2,128)S(1)} all-gather(f32[1,2,32]{2,1,0:T(2,128)S(1)} %bitcast.130), channel_id=3, replica_groups=mesh['dp'=2,'tok'=4,'exp'=4] {'tok'}, dimensions={0}, use_global_device_ids=true | all-gather | bytes 1280 | tf_op jit(solution)/shard_map/all_gather | solution.py:8
  20.5 8.1 %all-gather.3 = f32[4,2,32]{2,1,0:T(2,128)S(1)} all-gather(f32[1,2,32]{2,1,0:T(2,128)S(1)} %bitcast.129), channel_id=2, replica_groups=mesh['dp'=2,'tok'=4,'exp'=4] {'tok'}, dimensions={0}, use_global_device_ids=true | all-gather | bytes 1280 | tf_op jit(solution)/shard_map/all_gather | solution.py:8
  28.5 13.8 %all-gather.7.cloned.1.call-done = f32[8,32,1280]{2,1,0:T(8,128)} async-done(((f32[2,32,1280]{2,1,0:T(8,128)}), f32[8,32,1280]{2,1,0:T(8,128)}) %all-gather.7.cloned.1.call-update) | async-done | bytes 1310736 | tf_op jit(solution)/shard_map/all_gather | solution.py:8
  42.3 1.0 slice.10
  43.3 3.5 %while.19 = (s32[]{:T(128)}, f32[2,32]{1,0:T(2,128)S(1)}, f32[2,32]{1,0:T(2,128)S(1)}, f32[2,32,1280]{2,1,0:T(8,128)S(1)}, f32[4,2,32]{2,1,0:T(2,128)S(1)}, /*in...) while((s32[]{:T(128)}, f32[2,32]{1,0:T(2,128)S(1)}, ...), condition=%wide.region_6.7_spmd, body=%wide.region_5.6_spmd.sunk | while | flops 246149 | bytes 985751 | solution.py:13
  43.3 1.1 fusion.121
  44.5 1.1 fusion.121
  45.6 1.1 fusion.121
  46.8 0.1 divide_convert_fusion
  46.9 0.2 copy.19
  47.0 11.4 %all_to_all.36 = bf16[2,32,1280]{2,0,1:T(2,128)(2,1)S(1)} all-to-all(bf16[2,32,1280]{2,0,1:T(2,128)(2,1)S(1)} %copy.19), channel_id=1, replica_groups=mesh['dp'=2,'tok'=4,'exp'=4] {'exp'}, dimensions={1} | all-to-all | bytes 327680 | tf_op jit(solution)/shard_map/all_to_all | solution.py:47
  58.4 0.1 copy.28
  58.5 0.1 all_to_all.29
  58.6 15.8 %convolution_bitcast_fusion = f32[8,8,1280]{2,0,1:T(8,128)S(1)} fusion(bf16[8,1024,1280]{2,1,0:T(8,128)(2,1)} %param.13, bf16[8,8,1280]{2,0,1:T(8,128)(2,1)S(1)} %all_to_all.29, bf16[8,1280,1024]{2,1,0:T(8,128)(2,1)} %param.12), kind=kOutput, calls=%fused_computation.12 | convolution fusion | flops 339804160 | bytes 42434560 | tf_op jit(solution)/shard_map/bef,efd->bed/dot_general | solution.py:52
  74.4 21.3 %all-reduce.1 = bf16[8,8,1280]{2,0,1:T(8,128)(2,1)S(1)} all-reduce(f32[8,8,1280]{2,0,1:T(8,128)S(1)} %convolution_bitcast_fusion), channel_id=1, replica_groups=mesh['dp'=2,'tok'=4,'exp'=4] {'tok'}, use_global_device_ids=true, to_apply=%region_7.8 | all-reduce | flops 81920 | bytes 491520 | tf_op jit(solution)/shard_map/psum | solution.py:53
  95.6 0.7 copy.21
  96.3 3.3 %all-to-all-start.1 = ((bf16[8,8,1280]{2,1,0:T(8,128)(2,1)}), bf16[8,8,1280]{2,1,0:T(8,128)(2,1)S(1)}, u32[]{:S(2)}, u32[]{:S(2)}) async-start(bf16[8,8,1280]{2,1,0:T(8,128)(2,1)} %copy.21), calls=%async_computation.1 | async-start | bytes 327680 | tf_op jit(solution)/shard_map/all_to_all | solution.py:54
  99.7 5.9 %all-to-all-done.1 = bf16[8,8,1280]{2,1,0:T(8,128)(2,1)S(1)} async-done(((bf16[8,8,1280]{2,1,0:T(8,128)(2,1)}), bf16[8,8,1280]{2,1,0:T(8,128)(2,1)S(1)}, u32[]{:S(2)}, u32[]{:S(2)}) %all-to-all-start.1) | async-done | bytes 163872 | tf_op jit(solution)/shard_map/all_to_all | solution.py:54
  105.7 1.6 %fusion.4 = bf16[2,256,1280]{2,1,0:T(8,128)(2,1)} fusion(pred[2,256]{1,0:T(4,128)(4,1)S(1)} %and_reduce_fusion, bf16[4,2,8,1280]{3,2,1,0:T(8,128)(2,1)S(1)} %bitcast.128, f32[2,256]{1,0:T(2,128)S(1)} %fusion.101, f32[2,256,32]{1,2,0:T(8,128)S(1)} %get-tuple-element.203), kind=kOutput, calls=%fused_computation.11 | convolution fusion | flops 43303456 | bytes 1542656 | tf_op jit(solution)/shard_map/bns,bsd->bnd/dot_general | solution.py:58
  (7 shorter events, 0.1 us)
Async XLA Ops:
  6.5 1.6 %copy-start = (bf16[2,256,1280]{2,1,0:T(8,128)(2,1)S(1)}, bf16[2,256,1280]{2,1,0:T(8,128)(2,1)}, u32[]{:S(2)}) copy-start(bf16[2,256,1280]{2,1,0:T(8,128)(2,1)} %param.8) | copy-start | bytes 3932164
  6.5 35.7 %all-gather.7.cloned.1.call-start = ((), (), s32[]{:S(2)}) async-start(), calls=%async_computation.2 | async-start | bytes 1638400 | tf_op jit(solution)/shard_map/all_gather | solution.py:8
  96.3 9.3 %all-to-all-start.1 = ((bf16[8,8,1280]{2,1,0:T(8,128)(2,1)}), bf16[8,8,1280]{2,1,0:T(8,128)(2,1)S(1)}, u32[]{:S(2)}, u32[]{:S(2)}) async-start(bf16[8,8,1280]{2,1,0:T(8,128)(2,1)} %copy.21), calls=%async_computation.1 | async-start | bytes 327680 | tf_op jit(solution)/shard_map/all_to_all | solution.py:54
Sparse Core Ops, SparseCore 0:
  10.8 31.3 all-gather.6
where the time goes:
time: 115 us; the launch traced here: 114 us
  blocking collectives  50.2 us (44%)
  matrix products  20 us (17%)
  waiting for transfers between devices  19.7 us (17%)
  between operations  13.5 us (12%)
  other arithmetic  5.26 us (5%)
  starting transfers between devices  3.35 us (3%)
  local copies, waits for them, and re-layouts  2.05 us (2%)
    psum x1, blocking collectives, shards(): summed = lax.psum(partial_out, 'tok')  21.3 us
    all_gather x2, blocking collectives, combined_all(): gathered = jax.tree.map(lambda a: lax.all_gather(a, axis), part)  17.6 us
    dot_general x1, matrix products, shards(): jnp.einsum('bef,efd->bed', hidden, expert_out, preferred_element_type=jnp...  15.8 us
    all_gather x1, waiting for transfers between devices, combined_all(): gathered = jax.tree.map(lambda a: lax.all_gather(a, axis), part)  13.8 us
    all_to_all x1, blocking collectives, shards(): lax.all_to_all(slot_in, 'exp', split_axis=1, concat_axis=0, tiled=True)  11.4 us
    all_to_all x1, waiting for transfers between devices, shards(): lax.all_to_all(summed.astype(jnp.bfloat16), 'exp', split_axis=0, concat_a...  5.93 us
    all_to_all x1, starting transfers between devices, shards(): lax.all_to_all(summed.astype(jnp.bfloat16), 'exp', split_axis=0, concat_a...  3.35 us
    add x3, other arithmetic, merge_parts(): earlier[2] * first_scale[..., None]  3.31 us
  transfers between devices with their start and end apart: 2, of which 2 were waited for; matrix products, arithmetic and copies ran while one was open for 0% of the time, Pallas kernels for 0%

commit v1 on v0

--- a/solution.py
+++ b/solution.py
@@ -50,7 +50,8 @@
         approximate=False,
     ).astype(jnp.bfloat16)
     partial_out = jnp.einsum("bef,efd->bed", hidden, expert_out, preferred_element_type=jnp.float32)
-    summed = lax.psum(partial_out, "tok")
+    pieces = lax.all_gather(partial_out, "tok", axis=0, tiled=False)
+    summed = pieces.sum(axis=0)
     slot_out = lax.all_to_all(
         summed.astype(jnp.bfloat16), "exp", split_axis=0, concat_axis=1, tiled=True
     )

time: 115 us -> 124 us (1.078)
  waiting for transfers between devices: 19.7 us -> 46.7 us
  blocking collectives: 50.2 us -> 29 us
  other arithmetic: 5.26 us -> 6.66 us
  starting transfers between devices: 3.35 us -> 4.64 us
    all_gather x0 -> x1, waiting for transfers between devices: none -> 26.6 us  [shards(): pieces = lax.all_gather(partial_out, 'tok', axis=0, tiled=False)]
    psum x1 -> x0, blocking collectives: 21.3 us -> none  [shards(): summed = lax.psum(partial_out, 'tok')]
    reduce_sum x0 -> x1, other arithmetic: none -> 1.4 us  [shards(): summed = pieces.sum(axis=0)]
    all_to_all x1, starting transfers between devices: 3.35 us -> 4.6 us  [shards(): lax.all_to_all(summed.astype(jnp.bfloat16), 'exp', split_axis=0, concat_a...]
  transfers between devices with their start and end apart: 2 -> 3, of which waited for: 2 -> 3; matrix products, arithmetic and copies ran while one was open for 0% -> 0% of each run, Pallas kernels for 0% -> 0%
where the time goes in v1:
time: 124 us; the launch traced here: 123 us
  waiting for transfers between devices  46.7 us (38%)
  blocking collectives  29 us (23%)
  matrix products  20.8 us (17%)
  between operations  13.5 us (11%)
  other arithmetic  6.66 us (5%)
  starting transfers between devices  4.64 us (4%)
  local copies, waits for them, and re-layouts  2.05 us (2%)
    all_gather x1, waiting for transfers between devices, shards(): pieces = lax.all_gather(partial_out, 'tok', axis=0, tiled=False)  26.6 us
    all_gather x2, blocking collectives, combined_all(): gathered = jax.tree.map(lambda a: lax.all_gather(a, axis), part)  17.6 us
    dot_general x1, matrix products, shards(): jnp.einsum('bef,efd->bed', hidden, expert_out, preferred_element_type=jnp...  16.6 us
    all_gather x1, waiting for transfers between devices, combined_all(): gathered = jax.tree.map(lambda a: lax.all_gather(a, axis), part)  13.7 us
    all_to_all x1, blocking collectives, shards(): lax.all_to_all(slot_in, 'exp', split_axis=1, concat_axis=0, tiled=True)  11.4 us
    all_to_all x1, waiting for transfers between devices, shards(): lax.all_to_all(summed.astype(jnp.bfloat16), 'exp', split_axis=0, concat_a...  6.38 us
    all_to_all x1, starting transfers between devices, shards(): lax.all_to_all(summed.astype(jnp.bfloat16), 'exp', split_axis=0, concat_a...  4.6 us
    add x3, other arithmetic, merge_parts(): earlier[2] * first_scale[..., None]  3.31 us
  transfers between devices with their start and end apart: 3, of which 3 were waited for; matrix products, arithmetic and copies ran while one was open for 0% of the time, Pallas kernels for 0%

profile of v1, /device:TPU:0, one launch (start us, length us, event | category | flops | bytes accessed | tf_op | source)
XLA Modules:
  0.0 123.4 jit_solution(3227964772109760489)
XLA Ops:
  6.5 0.0 copy-start
  6.5 0.0 all-gather.9.cloned.1.call-start
  6.5 0.8 add.75
  7.3 0.8 and_reduce_fusion
  8.1 0.0 copy-done
  8.1 1.5 %select_reduce_fusion = (f32[2,32]{1,0:T(2,128)S(1)}, f32[2,256,32]{1,2,0:T(8,128)S(1)}) fusion(pred[2,256]{1,0:T(4,128)(4,1)S(1)} %and_reduce_fusion, bf16[2,256,1280]{2,1,0:T(8,128)(2,1)S(1)} %copy-done, bf16[1280,32]{0,1:T(8,128)(2,1)} %param.9), kind=kOutput, calls=%fused_computation.77 | convolution fusion | flops 41975744 | bytes 1458944 | tf_op jit(solution)/shard_map/bnd,ds->bns/dot_general | solution.py:35
  9.6 1.1 fusion.62
  10.7 0.0 all-gather.9.cloned.1.call-update
  10.7 0.0 all-gather.11.cloned.1.call-start
  10.8 0.2 fusion.61
  10.9 9.6 %all-gather.5 = f32[4,2,32]{2,1,0:T(2,128)S(1)} all-gather(f32[1,2,32]{2,1,0:T(2,128)S(1)} %bitcast.132), channel_id=3, replica_groups=mesh['dp'=2,'tok'=4,'exp'=4] {'tok'}, dimensions={0}, use_global_device_ids=true | all-gather | bytes 1280 | tf_op jit(solution)/shard_map/all_gather | solution.py:8
  20.5 8.1 %all-gather.4 = f32[4,2,32]{2,1,0:T(2,128)S(1)} all-gather(f32[1,2,32]{2,1,0:T(2,128)S(1)} %bitcast.131), channel_id=2, replica_groups=mesh['dp'=2,'tok'=4,'exp'=4] {'tok'}, dimensions={0}, use_global_device_ids=true | all-gather | bytes 1280 | tf_op jit(solution)/shard_map/all_gather | solution.py:8
  28.6 13.7 %all-gather.9.cloned.1.call-done = f32[8,32,1280]{2,1,0:T(8,128)} async-done(((f32[2,32,1280]{2,1,0:T(8,128)}), f32[8,32,1280]{2,1,0:T(8,128)}) %all-gather.9.cloned.1.call-update) | async-done | bytes 1310736 | tf_op jit(solution)/shard_map/all_gather | solution.py:8
  42.3 1.0 slice.10
  43.3 3.5 %while.19 = (s32[]{:T(128)}, f32[2,32]{1,0:T(2,128)S(1)}, f32[2,32]{1,0:T(2,128)S(1)}, f32[2,32,1280]{2,1,0:T(8,128)S(1)}, f32[4,2,32]{2,1,0:T(2,128)S(1)}, /*in...) while((s32[]{:T(128)}, f32[2,32]{1,0:T(2,128)S(1)}, ...), condition=%wide.region_6.7_spmd, body=%wide.region_5.6_spmd.sunk | while | flops 246149 | bytes 985751 | solution.py:13
  43.3 1.1 fusion.121
  44.5 1.1 fusion.121
  45.6 1.1 fusion.121
  46.8 0.1 divide_convert_fusion
  46.9 0.2 copy.25
  47.0 11.4 %all_to_all.36 = bf16[2,32,1280]{2,0,1:T(2,128)(2,1)S(1)} all-to-all(bf16[2,32,1280]{2,0,1:T(2,128)(2,1)S(1)} %copy.25), channel_id=1, replica_groups=mesh['dp'=2,'tok'=4,'exp'=4] {'exp'}, dimensions={1} | all-to-all | bytes 327680 | tf_op jit(solution)/shard_map/all_to_all | solution.py:47
  58.4 0.1 copy.34
  58.5 0.1 all_to_all.29
  58.6 16.6 %convolution_bitcast_fusion = f32[8,8,1280]{2,0,1:T(8,128)} fusion(bf16[8,1024,1280]{2,1,0:T(8,128)(2,1)} %param.13, bf16[8,8,1280]{2,0,1:T(8,128)(2,1)S(1)} %all_to_all.29, bf16[8,1280,1024]{2,1,0:T(8,128)(2,1)} %param.12), kind=kOutput, calls=%fused_computation.12 | convolution fusion | flops 339804160 | bytes 42434560 | tf_op jit(solution)/shard_map/bef,efd->bed/dot_general | solution.py:52
  75.2 0.0 all-gather.11.cloned.1.call-update
  75.2 26.6 %all-gather.11.cloned.1.call-done = f32[32,8,1280]{2,0,1:T(8,128)} async-done(((f32[8,8,1280]{2,0,1:T(8,128)}), f32[32,8,1280]{2,0,1:T(8,128)}) %all-gather.11.cloned.1.call-update) | async-done | bytes 1310736 | tf_op jit(solution)/shard_map/all_gather | solution.py:53
  101.8 1.4 %bitcast_reduce_fusion = bf16[8,8,1280]{2,0,1:T(8,128)(2,1)S(1)} fusion(f32[32,8,1280]{2,0,1:T(8,128)} %all-gather.11.cloned.1.call-done), kind=kLoop, calls=%fused_computation.13 | loop fusion | flops 245760 | bytes 1474560 | tf_op jit(solution)/shard_map/reduce_sum | solution.py:54
  103.2 0.7 copy.27
  103.9 4.6 %all-to-all-start.1 = ((bf16[8,8,1280]{2,1,0:T(8,128)(2,1)}), bf16[8,8,1280]{2,1,0:T(8,128)(2,1)S(1)}, u32[]{:S(2)}, u32[]{:S(2)}) async-start(bf16[8,8,1280]{2,1,0:T(8,128)(2,1)} %copy.27), calls=%async_computation.1 | async-start | bytes 327680 | tf_op jit(solution)/shard_map/all_to_all | solution.py:55
  108.6 6.4 %all-to-all-done.1 = bf16[8,8,1280]{2,1,0:T(8,128)(2,1)S(1)} async-done(((bf16[8,8,1280]{2,1,0:T(8,128)(2,1)}), bf16[8,8,1280]{2,1,0:T(8,128)(2,1)S(1)}, u32[]{:S(2)}, u32[]{:S(2)}) %all-to-all-start.1) | async-done | bytes 163872 | tf_op jit(solution)/shard_map/all_to_all | solution.py:55
  115.0 1.6 %fusion.4 = bf16[2,256,1280]{2,1,0:T(8,128)(2,1)} fusion(pred[2,256]{1,0:T(4,128)(4,1)S(1)} %and_reduce_fusion, bf16[2,4,8,1280]{3,2,0,1:T(8,128)(2,1)S(1)} %bitcast.130, f32[2,256]{1,0:T(2,128)S(1)} %fusion.101, f32[2,256,32]{1,2,0:T(8,128)S(1)} %get-tuple-element.203), kind=kOutput, calls=%fused_computation.11 | convolution fusion | flops 43303456 | bytes 1542656 | tf_op jit(solution)/shard_map/bns,bsd->bnd/dot_general | solution.py:59
  (7 shorter events, 0.1 us)
Async XLA Ops:
  6.5 1.6 %copy-start = (bf16[2,256,1280]{2,1,0:T(8,128)(2,1)S(1)}, bf16[2,256,1280]{2,1,0:T(8,128)(2,1)}, u32[]{:S(2)}) copy-start(bf16[2,256,1280]{2,1,0:T(8,128)(2,1)} %param.8) | copy-start | bytes 3932164
  6.5 35.7 %all-gather.9.cloned.1.call-start = ((), (), s32[]{:S(2)}) async-start(), calls=%async_computation.2 | async-start | bytes 1638400 | tf_op jit(solution)/shard_map/all_gather | solution.py:8
  10.7 91.1 %all-gather.11.cloned.1.call-start = ((), (), s32[]{:S(2)}) async-start(), calls=%async_computation.3 | async-start | bytes 1638400 | tf_op jit(solution)/shard_map/all_gather | solution.py:53
  103.9 11.0 %all-to-all-start.1 = ((bf16[8,8,1280]{2,1,0:T(8,128)(2,1)}), bf16[8,8,1280]{2,1,0:T(8,128)(2,1)S(1)}, u32[]{:S(2)}, u32[]{:S(2)}) async-start(bf16[8,8,1280]{2,1,0:T(8,128)(2,1)} %copy.27), calls=%async_computation.1 | async-start | bytes 327680 | tf_op jit(solution)/shard_map/all_to_all | solution.py:55
Sparse Core Ops, SparseCore 0:
  10.8 31.3 all-gather.8
  75.4 26.4 all-gather.10
